TPU v7x, 128 devices: a whole 4x4x4 slice. The times are simulated.
128 devices in a mesh: sub: 8 (over z, core), row: 4 (over x), col: 4 (over y).
Axes of the slice: x: 4, y: 4, z: 4, core: 2. Of those that a mesh axis runs over, the one named last changes fastest.
Arguments:
- front: float32 [4, 32, 128, 32, 4, 128], P(None, ('sub', 'row'), None, None, 'col'), may hold values from -2.4 to 7.5, as said below
- child_tiles: bfloat16 [16384, 128, 128], P(('sub', 'row', 'col')), may hold values from -2.390625 to 2.390625
- tile_owner: int32 [16384, 1], P(('sub', 'row', 'col')), may hold values from 0 to 127; in each aligned block of 128 rows (0 to 127, 128 to 255, ...) at most 2 rows name the same one
- tile_slot: int32 [16384], P(('sub', 'row', 'col')), may hold values from 2 to 127
Outputs:
- updated: float32 [4, 32, 128, 32, 4, 128], P(None, ('sub', 'row'), None, None, 'col')
- panel: bfloat16 [4, 32, 128, 2, 4, 128], P(None, ('sub', 'row'), None, None, 'col')
Inputs may be any that keep to these rules, and one draw needn't show every extreme that they name: The leading 1024 x 1024 block of front, made symmetric from its lower triangle, is positive definite. `tile_owner`: at most 2 of the tiles of one device go to one owner.
All inputs are finite; a program needn't handle non-finite values.
Results may differ from a plain program's by a relative error of at most 0.0038.
Values may be sent and summed in bfloat16 or wider, within the bound.
A program may use at most 128 MiB of HBM per device.

v0:
```python
import jax
import jax.numpy as jnp
from jax import lax
from jax.sharding import PartitionSpec as P

NB = 1024


def broadcast(block, axis, source):
    block = jnp.where(lax.axis_index(axis) == source, block, jnp.zeros_like(block))
    return lax.psum(block, axis)


def local(front, child_tiles, tile_owner, tile_slot):
    row_tiles, _, tile_size, col_tiles, _, _ = front.shape
    sub_count = lax.axis_size("sub")
    row_count = lax.axis_size("row")
    col_count = lax.axis_size("col")
    dev_count = sub_count * row_count * col_count
    tile_count = child_tiles.shape[0]
    capacity = max(2, 2 * tile_count // dev_count)
    panel_tiles = NB // tile_size
    per_col = panel_tiles // col_count
    height = row_tiles * tile_size
    local_front = front.reshape(row_tiles, tile_size, col_tiles, tile_size)
    owners = tile_owner[:, 0]
    matches = (owners[:, None] == jnp.arange(dev_count, dtype=jnp.int32)[None, :]).astype(jnp.int32)
    before = jnp.cumsum(matches, 0) - matches
    placed = jnp.sum(before * matches, 1)
    outgoing = (
        jnp.zeros((dev_count, capacity, tile_size, tile_size), jnp.bfloat16)
        .at[owners, placed]
        .set(child_tiles)
    )
    targets = jnp.full((dev_count, capacity), -1, jnp.int32).at[owners, placed].set(tile_slot)
    arrived, landing = (
        lax.all_to_all(outgoing, ("sub", "row", "col"), split_axis=0, concat_axis=0, tiled=True),
        lax.all_to_all(targets, ("sub", "row", "col"), split_axis=0, concat_axis=0, tiled=True),
    )
    arrived = arrived.reshape(dev_count * capacity, tile_size, tile_size)
    landing = landing.reshape(dev_count * capacity)
    selector = (
        landing[:, None] == jnp.arange(row_tiles * col_tiles, dtype=jnp.int32)[None, :]
    ).astype(jnp.bfloat16)
    selector = selector.reshape(dev_count * capacity, row_tiles, col_tiles)
    assembled = local_front + jnp.einsum(
        "kqs,kab->qasb", selector, arrived, preferred_element_type=jnp.float32
    )
    sub_index = lax.axis_index("sub")
    row_index = lax.axis_index("row")
    col_index = lax.axis_index("col")
    group_id = sub_index * row_count + row_index
    corner = assembled[0, :, :per_col, :]
    beside_all = lax.all_gather(corner, ("row", "col"), axis=0, tiled=True)
    beside_all = beside_all.reshape(row_count, col_count, tile_size, per_col, tile_size)
    beside_all = beside_all.transpose(0, 2, 3, 1, 4).reshape(row_count * tile_size, NB)
    blocks = []
    for owner_sub in range(panel_tiles // row_count):
        blocks.append(broadcast(beside_all, "sub", owner_sub))
    pivot = jnp.concatenate(blocks, 0)
    symmetric = jnp.tril(pivot) + jnp.tril(pivot, -1).T
    factor = jnp.linalg.cholesky(symmetric)
    panel_cols = assembled[:, :, :per_col, :].reshape(height, per_col, 1, tile_size)
    widened = lax.all_gather(panel_cols, "col", axis=2, tiled=True).reshape(height, NB)
    solved = jax.scipy.linalg.solve_triangular(factor, widened.T, lower=True).T.astype(jnp.bfloat16)
    leading = lax.dynamic_slice_in_dim(
        factor, jnp.minimum(group_id, panel_tiles - 1) * tile_size, tile_size, 0
    ).astype(jnp.bfloat16)
    upper = jnp.where(group_id < panel_tiles, leading, solved[:tile_size])
    panel_rows = jnp.concatenate([upper, solved[tile_size:]], 0)
    panel_out = lax.dynamic_index_in_dim(
        panel_rows.reshape(row_tiles, tile_size, per_col, col_count, tile_size),
        col_index,
        3,
        keepdims=True,
    )
    panel_out = panel_out.reshape(row_tiles, 1, tile_size, per_col, 1, tile_size)
    across = broadcast(panel_rows, "row", col_index)
    update = jnp.einsum(
        "rk,nqbk->rqnb",
        panel_rows,
        lax.all_gather(across.reshape(1, row_tiles, tile_size, NB), "sub", axis=0, tiled=True),
        preferred_element_type=jnp.float32,
    )
    update = update.reshape(row_tiles, tile_size, col_tiles, tile_size)
    row_tile = jnp.arange(row_tiles, dtype=jnp.int32) * (row_count * sub_count) + group_id
    col_tile = jnp.arange(col_tiles, dtype=jnp.int32) * col_count + col_index
    trailing_mask = (row_tile >= panel_tiles)[:, None, None, None] & (col_tile >= panel_tiles)[
        None, None, :, None
    ]
    result = jnp.where(trailing_mask, assembled - update, assembled)
    return (result.reshape(front.shape), panel_out)


def solution(mesh):
    return jax.shard_map(
        local,
        mesh=mesh,
        in_specs=(
            P(None, ("sub", "row"), None, None, "col", None),
            P(("sub", "row", "col"), None, None),
            P(("sub", "row", "col"), None),
            P(("sub", "row", "col")),
        ),
        out_specs=(
            P(None, ("sub", "row"), None, None, "col", None),
            P(None, ("sub", "row"), None, None, "col", None),
        ),
        check_vma=False,
    )
```

profile of v0, /device:TPU:1, one launch (start us, length us, event | category | flops | bytes accessed | tf_op | source)
XLA Modules:
  0.0 870.7 jit_solution(1453275617700814061)
XLA Ops:
  9.6 11.0 %scatter_fusion.1 = s32[128,2]{0,1:T(2,128)S(1)} fusion(s32[128,2]{0,1:T(2,128)S(1)} %broadcast_in_dim.35, s32[128]{0:T(128)S(1)} %fusion.70, s32[128]{0:T(128)} %param.7), kind=kCustom, calls=%fused_computation.1 | custom fusion | bytes 2560 | tf_op jit(solution)/shard_map/scatter | solution.py:35
  21.3 11.5 %all-to-all-start.1 = ((s32[128,1,2]{2,1,0:T(1,128)}), s32[128,1,2]{2,1,0:T(1,128)S(1)}, u32[]{:S(2)}, u32[]{:S(2)}) async-start(s32[128,1,2]{2,1,0:T(1,128)} %copy.65), calls=%async_computation.1 | async-start | bytes 131072 | tf_op jit(solution)/shard_map/all_to_all | solution.py:38
  38.3 20.7 %scatter_fusion = bf16[128,2,128,128]{3,2,1,0:T(8,128)(2,1)} fusion(bf16[128,2,128,128]{3,2,1,0:T(8,128)(2,1)} %broadcast_in_dim.34, s32[128]{0:T(128)S(1)} %fusion.70, bf16[128,128,128]{2,1,0:T(8,128)(2,1)} %param.5), kind=kCustom, calls=%fused_computation | custom fusion | bytes 12583936 | tf_op jit(solution)/shard_map/scatter | solution.py:33
  59.1 10.2 %all-to-all-start = ((bf16[128,2,128,128]{3,2,1,0:T(8,128)(2,1)}), bf16[128,2,128,128]{3,2,1,0:T(8,128)(2,1)}, u32[]{:S(2)}, u32[]{:S(2)}) async-start(bf16[128,2,128,128]{3,2,1,0:T(8,128)(2,1)} %scatter_fusion), calls=%async_computation | async-start | bytes 16777216 | tf_op jit(solution)/shard_map/all_to_all | solution.py:37
  70.8 99.1 %all-to-all-done = bf16[128,2,128,128]{3,2,1,0:T(8,128)(2,1)} async-done(((bf16[128,2,128,128]{3,2,1,0:T(8,128)(2,1)}), bf16[128,2,128,128]{3,2,1,0:T(8,128)(2,1)}, u32[]{:S(2)}, u32[]{:S(2)}) %all-to-all-start) | async-done | bytes 8388640 | tf_op jit(solution)/shard_map/all_to_all | solution.py:37
  169.9 12.2 %copy.64 = bf16[128,2,128,128]{3,1,0,2:T(2,128)(2,1)S(1)} copy(bf16[128,2,128,128]{3,2,1,0:T(8,128)(2,1)} %all-to-all-done) | data formatting | bytes 16777216 | tf_op jit(solution)/shard_map/all_to_all | solution.py:37
  194.4 40.8 %all-gather.9.cloned.1.call-done = f32[1,2048,2,128]{3,2,0,1:T(2,128)} async-done(((f32[1,128,2,128]{3,2,0,1:T(2,128)}), f32[1,2048,2,128]{3,2,0,1:T(2,128)}) %all-gather.9.cloned.1.call-update) | async-done | bytes 2097168 | tf_op jit(solution)/shard_map/all_gather | solution.py:54
  249.6 18.8 %all-gather.5.cloned.1.call-done = f32[512,2,4,128]{3,0,1,2:T(8,128)} async-done(((f32[512,2,1,128]{3,0,1,2:T(8,128)}), f32[512,2,4,128]{3,0,1,2:T(8,128)}) %all-gather.5.cloned.1.call-update) | async-done | bytes 2097168 | tf_op jit(solution)/shard_map/all_gather | solution.py:64
  270.4 71.8 %all-reduce.7.cloned.1.call-done = (f32[512,1024]{1,0:T(8,128)}, f32[512,1024]{1,0:T(8,128)}) async-done(((f32[512,1024]{1,0:T(8,128)}, f32[512,1024]{1,0:T(8,128)}), (f32[512,1024]{1,0:T(8,128)}, f32[512,1024]{1,0:T(8,128)})) %all-reduce.7.cloned.1.call-update) | async-done | bytes 4194320 | tf_op jit(solution)/shard_map/psum | solution.py:11
  372.2 11.7 %cholesky.222 = f32[128,128]{1,0:T(8,128)S(1)} custom-call(f32[128,128]{1,0:T(8,128)S(1)} %cholesky.577), custom_call_target="Cholesky" | custom-call | tf_op jit(solution)/shard_map/jit(cholesky)/cholesky | solution.py:62
  386.5 9.8 %custom-call.63 = f32[1,128,128]{1,2,0:T(8,128)S(1)} custom-call(f32[1,128,128]{2,1,0:T(8,128)S(1)} %get-tuple-element.74), custom_call_target="InvertDiagBlocksLowerTriangular" | custom-call | tf_op jit(solution)/shard_map/jit(cholesky)/cholesky | solution.py:62
  400.2 12.1 %cholesky.243 = f32[128,128]{1,0:T(8,128)S(1)} custom-call(f32[128,128]{1,0:T(8,128)S(1)} %cholesky.581), custom_call_target="Cholesky" | custom-call | tf_op jit(solution)/shard_map/jit(cholesky)/cholesky | solution.py:62
  413.0 9.8 %custom-call.64 = f32[1,128,128]{1,2,0:T(8,128)S(1)} custom-call(f32[1,128,128]{2,1,0:T(8,128)S(1)} %get-tuple-element.71), custom_call_target="InvertDiagBlocksLowerTriangular" | custom-call | tf_op jit(solution)/shard_map/jit(cholesky)/cholesky | solution.py:62
  426.1 11.7 %cholesky.466 = f32[128,128]{1,0:T(8,128)S(1)} custom-call(f32[128,128]{1,0:T(8,128)S(1)} %cholesky.586), custom_call_target="Cholesky" | custom-call | tf_op jit(solution)/shard_map/jit(cholesky)/cholesky | solution.py:62
  439.1 9.8 %custom-call.65 = f32[1,128,128]{1,2,0:T(8,128)S(1)} custom-call(f32[1,128,128]{2,1,0:T(8,128)S(1)} %get-tuple-element.68), custom_call_target="InvertDiagBlocksLowerTriangular" | custom-call | tf_op jit(solution)/shard_map/jit(cholesky)/cholesky | solution.py:62
  452.4 11.8 %cholesky.485 = f32[128,128]{1,0:T(8,128)S(1)} custom-call(f32[128,128]{1,0:T(8,128)S(1)} %cholesky.591), custom_call_target="Cholesky" | custom-call | tf_op jit(solution)/shard_map/jit(cholesky)/cholesky | solution.py:62
  465.6 9.8 %custom-call.66 = f32[1,128,128]{1,2,0:T(8,128)S(1)} custom-call(f32[1,128,128]{2,1,0:T(8,128)S(1)} %get-tuple-element.65), custom_call_target="InvertDiagBlocksLowerTriangular" | custom-call | tf_op jit(solution)/shard_map/jit(cholesky)/cholesky | solution.py:62
  478.8 11.7 %cholesky.504 = f32[128,128]{1,0:T(8,128)S(1)} custom-call(f32[128,128]{1,0:T(8,128)S(1)} %cholesky.596), custom_call_target="Cholesky" | custom-call | tf_op jit(solution)/shard_map/jit(cholesky)/cholesky | solution.py:62
  491.8 10.0 %custom-call.67 = f32[1,128,128]{1,2,0:T(8,128)S(1)} custom-call(f32[1,128,128]{2,1,0:T(8,128)S(1)} %get-tuple-element.62), custom_call_target="InvertDiagBlocksLowerTriangular" | custom-call | tf_op jit(solution)/shard_map/jit(cholesky)/cholesky | solution.py:62
  505.2 11.7 %cholesky.524 = f32[128,128]{1,0:T(8,128)S(1)} custom-call(f32[128,128]{1,0:T(8,128)S(1)} %cholesky.601), custom_call_target="Cholesky" | custom-call | tf_op jit(solution)/shard_map/jit(cholesky)/cholesky | solution.py:62
  518.1 9.8 %custom-call.68 = f32[1,128,128]{1,2,0:T(8,128)S(1)} custom-call(f32[1,128,128]{2,1,0:T(8,128)S(1)} %get-tuple-element.59), custom_call_target="InvertDiagBlocksLowerTriangular" | custom-call | tf_op jit(solution)/shard_map/jit(cholesky)/cholesky | solution.py:62
  531.0 12.1 %cholesky.544 = f32[128,128]{1,0:T(8,128)S(1)} custom-call(f32[128,128]{1,0:T(8,128)S(1)} %cholesky.606), custom_call_target="Cholesky" | custom-call | tf_op jit(solution)/shard_map/jit(cholesky)/cholesky | solution.py:62
  544.3 9.8 %custom-call.69 = f32[1,128,128]{1,2,0:T(8,128)S(1)} custom-call(f32[1,128,128]{2,1,0:T(8,128)S(1)} %get-tuple-element.56), custom_call_target="InvertDiagBlocksLowerTriangular" | custom-call | tf_op jit(solution)/shard_map/jit(cholesky)/cholesky | solution.py:62
  556.7 11.7 %cholesky.562 = f32[128,128]{1,0:T(8,128)S(1)} custom-call(f32[128,128]{1,0:T(8,128)S(1)} %convolution_subtract_fusion.13), custom_call_target="Cholesky" | custom-call | tf_op jit(solution)/shard_map/jit(cholesky)/cholesky | solution.py:62
  581.1 27.9 %while.1 = (s32[]{:T(128)}, f32[1024,1024]{1,0:T(8,128)}, s32[8,2]{0,1:T(2,128)S(1)}, f32[8,128,128]{2,1,0:T(8,128)}, s32[]{:T(128)}) while((s32[]{:T(128)}, f32[1024,1024]{1,0:T(8,128)}, s32[8,2]{0,1:T(2,128)S(1)}, f32[8,128,128]{2,1,0:T(8,128)}, s32[]{:T(128)}) %tuple.68), condition=%wide.while_cond, body=%wide.while_body.sunk | while | flops 2 | bytes 132705 | solution.py:65
  609.0 79.6 %custom-call.70 = f32[8,128,128]{1,2,0:T(8,128)S(1)} custom-call(f32[8,128,128]{2,1,0:T(8,128)} %get-tuple-element.9), custom_call_target="InvertDiagBlocksLowerTriangular" | custom-call | tf_op jit(solution)/shard_map/jit(_solve_triangular)/triangular_solve | solution.py:65
  719.9 45.9 %all-reduce.5.cloned.1.call-done = bf16[1,4,128,1024]{3,2,1,0:T(8,128)(2,1)} async-done(((bf16[1,4,128,1024]{3,2,1,0:T(8,128)(2,1)}), bf16[1,4,128,1024]{3,2,1,0:T(8,128)(2,1)}) %all-reduce.5.cloned.1.call-update) | async-done | bytes 1048592 | tf_op jit(solution)/shard_map/psum | solution.py:11
  768.5 52.0 %all-gather.7.cloned.1.call-done = bf16[8,4,128,1024]{3,2,1,0:T(8,128)(2,1)} async-done(((bf16[1,4,128,1024]{3,2,1,0:T(8,128)(2,1)}), bf16[8,4,128,1024]{3,2,1,0:T(8,128)(2,1)}) %all-gather.7.cloned.1.call-update) | async-done | bytes 8388624 | tf_op jit(solution)/shard_map/all_gather | solution.py:82
  820.5 10.4 %convolution_bitcast_fusion = f32[512,4,8,128]{0,3,1,2:T(8,128)} fusion(bf16[8,4,128,1024]{3,2,1,0:T(8,128)(2,1)} %all-gather.7.cloned.1.call-done, bf16[384,1024]{1,0:T(8,128)(2,1)S(1)} %slice.280, bf16[128,1024]{1,0:T(8,128)(2,1)S(1)} %fusion.36), kind=kOutput, calls=%fused_computation.15 | convolution fusion | flops 4297064448 | bytes 17825792 | tf_op jit(solution)/shard_map/rk,nqbk->rqnb/dot_general | solution.py:79
  830.8 10.4 %copy.80 = f32[512,4,8,128]{3,2,1,0:T(8,128)} copy(f32[512,4,8,128]{0,3,1,2:T(8,128)} %convolution_bitcast_fusion) | data formatting | bytes 16777216 | tf_op jit(solution)/shard_map/rk,nqbk->rqnb/transpose | solution.py:79
  841.3 11.7 %fusion = f32[4,1,128,32,1,128]{5,3,0,2,4,1:T(8,128)} fusion(f32[4,128,32,128]{3,2,0,1:T(8,128)} %copy-done, f32[4,128,32,128]{3,2,1,0:T(8,128)} %bitcast.154, pred[4,32]{1,0:T(4,128)(4,1)S(1)} %broadcast_and_fusion), kind=kLoop, calls=%fused_computation.5 | loop fusion | flops 4194304 | bytes 25165952 | tf_op jit(solution)/shard_map/reshape | solution.py:92
  853.0 11.0 %copy.83 = f32[4,1,128,32,1,128]{5,4,3,2,1,0:T(1,128)} copy(f32[4,1,128,32,1,128]{5,3,0,2,4,1:T(8,128)} %fusion) | data formatting | bytes 16777216
  (154 shorter events, 170.7 us)
Async XLA Ops:
  21.3 37.7 %all-to-all-start.1 = ((s32[128,1,2]{2,1,0:T(1,128)}), s32[128,1,2]{2,1,0:T(1,128)S(1)}, u32[]{:S(2)}, u32[]{:S(2)}) async-start(s32[128,1,2]{2,1,0:T(1,128)} %copy.65), calls=%async_computation.1 | async-start | bytes 131072 | tf_op jit(solution)/shard_map/all_to_all | solution.py:38
  59.1 110.8 %all-to-all-start = ((bf16[128,2,128,128]{3,2,1,0:T(8,128)(2,1)}), bf16[128,2,128,128]{3,2,1,0:T(8,128)(2,1)}, u32[]{:S(2)}, u32[]{:S(2)}) async-start(bf16[128,2,128,128]{3,2,1,0:T(8,128)(2,1)} %scatter_fusion), calls=%async_computation | async-start | bytes 16777216 | tf_op jit(solution)/shard_map/all_to_all | solution.py:37
  69.3 165.9 %all-gather.9.cloned.1.call-start = ((), (), s32[]{:S(2)}) async-start(), calls=%async_computation.5 | async-start | bytes 2228224 | tf_op jit(solution)/shard_map/all_gather | solution.py:54
  187.2 3.4 copy-start
  191.4 77.1 %all-gather.5.cloned.1.call-start = ((), (), s32[]{:S(2)}) async-start(), calls=%async_computation.2 | async-start | bytes 2621440 | tf_op jit(solution)/shard_map/all_gather | solution.py:64
  194.2 148.1 %all-reduce.7.cloned.1.call-start = ((), (), s32[]{:S(2)}) async-start(), calls=%async_computation.6 | async-start | bytes 8388608 | tf_op jit(solution)/shard_map/psum | solution.py:11
  249.5 516.3 %all-reduce.5.cloned.1.call-start = ((), (), s32[]{:S(2)}) async-start(), calls=%async_computation.3 | async-start | bytes 2097152 | tf_op jit(solution)/shard_map/psum | solution.py:11
  342.2 2.2 copy-start.3
  344.7 1.9 copy-start.1
  370.3 1.9 copy-start.2
  688.6 8.2 copy-start.4
  719.9 100.6 %all-gather.7.cloned.1.call-start = ((), (), s32[]{:S(2)}) async-start(), calls=%async_computation.4 | async-start | bytes 9437184 | tf_op jit(solution)/shard_map/all_gather | solution.py:82
Sparse Core Ops, SparseCore 0:
  191.5 43.6 all-gather.8
  236.9 31.5 all-gather.4
  270.9 71.2 all-reduce.6
  720.0 45.8 all-reduce.4
  767.4 53.0 all-gather.6
where the time goes:
time: 878 us; the launch traced here: 871 us
  waiting for transfers between devices  329 us (37%)
  other arithmetic  291 us (33%)
  local copies, waits for them, and re-layouts  144 us (16%)
  matrix products  66.1 us (8%)
  starting transfers between devices  22.1 us (3%)
  between operations  19.5 us (2%)
    another operation x30, other arithmetic, local(): factor = jnp.linalg.cholesky(symmetric)  172 us
    psum x2, waiting for transfers between devices, broadcast(): return lax.psum(block, axis)  118 us
    all_to_all x1, waiting for transfers between devices, local(): lax.all_to_all(outgoing, ('sub', 'row', 'col'), split_axis=0, concat_axis...  99.1 us
    another operation x3, other arithmetic, local(): jax.scipy.linalg.solve_triangular(factor, widened.T, lower=True)  85.4 us
    all_gather x1, waiting for transfers between devices, local(): lax.all_gather(across.reshape(1, row_tiles, tile_size, NB), 'sub', axis=0...  52 us
    all_gather x1, waiting for transfers between devices, local(): beside_all = lax.all_gather(corner, ('row', 'col'), axis=0, tiled=True)  40.8 us
    another operation x24, local copies, waits for them, and re-layouts  27.9 us
    another operation x15, matrix products, local(): jax.scipy.linalg.solve_triangular(factor, widened.T, lower=True)  27.5 us
  transfers between devices with their start and end apart: 7, of which 6 were waited for; matrix products, arithmetic and copies ran while one was open for 6% of the time, Pallas kernels for 0%

commit v1 on v0

--- a/solution.py
+++ b/solution.py
@@ -8,7 +8,7 @@
 
 def broadcast(block, axis, source):
     block = jnp.where(lax.axis_index(axis) == source, block, jnp.zeros_like(block))
-    return lax.psum(block, axis)
+    return jnp.sum(lax.all_gather(block, axis), axis=0)
 
 
 def local(front, child_tiles, tile_owner, tile_slot):

time: 878 us -> 987 us (1.12)
  waiting for transfers between devices: 329 us -> 419 us
  other arithmetic: 291 us -> 313 us
    all_gather x0 -> x3, waiting for transfers between devices: none -> 212 us  [broadcast(): return jnp.sum(lax.all_gather(block, axis), axis=0)]
    psum x2 -> x0, waiting for transfers between devices: 118 us -> none  [broadcast(): return lax.psum(block, axis)]
    reduce_sum x0 -> x3, other arithmetic: none -> 21.8 us  [broadcast(): return jnp.sum(lax.all_gather(block, axis), axis=0)]
    unnamed x21 -> x18, local copies, waits for them, and re-layouts: 21.7 us -> 18.5 us
  transfers between devices with their start and end apart: 7 -> 8, of which waited for: 6 -> 7; matrix products, arithmetic and copies ran while one was open for 6% -> 6% of each run, Pallas kernels for 0% -> 0%
where the time goes in v1:
time: 987 us; the launch traced here: 978 us
  waiting for transfers between devices  419 us (42%)
  other arithmetic  313 us (32%)
  local copies, waits for them, and re-layouts  137 us (14%)
  matrix products  66.9 us (7%)
  starting transfers between devices  22.2 us (2%)
  between operations  19.9 us (2%)
    all_gather x3, waiting for transfers between devices, broadcast(): return jnp.sum(lax.all_gather(block, axis), axis=0)  212 us
    another operation x30, other arithmetic, local(): factor = jnp.linalg.cholesky(symmetric)  172 us
    all_to_all x1, waiting for transfers between devices, local(): lax.all_to_all(outgoing, ('sub', 'row', 'col'), split_axis=0, concat_axis...  99.1 us
    another operation x3, other arithmetic, local(): jax.scipy.linalg.solve_triangular(factor, widened.T, lower=True)  84.7 us
    all_gather x1, waiting for transfers between devices, local(): lax.all_gather(across.reshape(1, row_tiles, tile_size, NB), 'sub', axis=0...  48.2 us
    all_gather x1, waiting for transfers between devices, local(): beside_all = lax.all_gather(corner, ('row', 'col'), axis=0, tiled=True)  41 us
    another operation x15, matrix products, local(): jax.scipy.linalg.solve_triangular(factor, widened.T, lower=True)  28.3 us
    another operation x14, matrix products, local(): factor = jnp.linalg.cholesky(symmetric)  23.1 us
  transfers between devices with their start and end apart: 8, of which 7 were waited for; matrix products, arithmetic and copies ran while one was open for 6% of the time, Pallas kernels for 0%

profile of v1, /device:TPU:1, one launch (start us, length us, event | category | flops | bytes accessed | tf_op | source)
XLA Modules:
  0.0 977.7 jit_solution(1868098901785842998)
XLA Ops:
  9.6 11.0 %scatter_fusion.1 = s32[128,2]{0,1:T(2,128)S(1)} fusion(s32[128,2]{0,1:T(2,128)S(1)} %broadcast_in_dim.35, s32[128]{0:T(128)S(1)} %fusion.70, s32[128]{0:T(128)} %param.7), kind=kCustom, calls=%fused_computation.1 | custom fusion | bytes 2560 | tf_op jit(solution)/shard_map/scatter | solution.py:35
  21.3 11.5 %all-to-all-start.1 = ((s32[128,1,2]{2,1,0:T(1,128)}), s32[128,1,2]{2,1,0:T(1,128)S(1)}, u32[]{:S(2)}, u32[]{:S(2)}) async-start(s32[128,1,2]{2,1,0:T(1,128)} %copy.63), calls=%async_computation.1 | async-start | bytes 131072 | tf_op jit(solution)/shard_map/all_to_all | solution.py:38
  38.3 20.7 %scatter_fusion = bf16[128,2,128,128]{3,2,1,0:T(8,128)(2,1)} fusion(bf16[128,2,128,128]{3,2,1,0:T(8,128)(2,1)} %broadcast_in_dim.34, s32[128]{0:T(128)S(1)} %fusion.70, bf16[128,128,128]{2,1,0:T(8,128)(2,1)} %param.5), kind=kCustom, calls=%fused_computation | custom fusion | bytes 12583936 | tf_op jit(solution)/shard_map/scatter | solution.py:33
  59.1 10.2 %all-to-all-start = ((bf16[128,2,128,128]{3,2,1,0:T(8,128)(2,1)}), bf16[128,2,128,128]{3,2,1,0:T(8,128)(2,1)}, u32[]{:S(2)}, u32[]{:S(2)}) async-start(bf16[128,2,128,128]{3,2,1,0:T(8,128)(2,1)} %scatter_fusion), calls=%async_computation | async-start | bytes 16777216 | tf_op jit(solution)/shard_map/all_to_all | solution.py:37
  70.8 99.1 %all-to-all-done = bf16[128,2,128,128]{3,2,1,0:T(8,128)(2,1)} async-done(((bf16[128,2,128,128]{3,2,1,0:T(8,128)(2,1)}), bf16[128,2,128,128]{3,2,1,0:T(8,128)(2,1)}, u32[]{:S(2)}, u32[]{:S(2)}) %all-to-all-start) | async-done | bytes 8388640 | tf_op jit(solution)/shard_map/all_to_all | solution.py:37
  169.9 12.2 %copy.62 = bf16[128,2,128,128]{3,1,0,2:T(2,128)(2,1)S(1)} copy(bf16[128,2,128,128]{3,2,1,0:T(8,128)(2,1)} %all-to-all-done) | data formatting | bytes 16777216 | tf_op jit(solution)/shard_map/all_to_all | solution.py:37
  194.2 41.0 %all-gather.18.cloned.1.call-done = f32[1,2048,2,128]{3,2,0,1:T(2,128)} async-done(((f32[1,128,2,128]{3,2,0,1:T(2,128)}), f32[1,2048,2,128]{3,2,0,1:T(2,128)}) %all-gather.18.cloned.1.call-update) | async-done | bytes 2097168 | tf_op jit(solution)/shard_map/all_gather | solution.py:54
  249.9 18.6 %all-gather.12.cloned.1.call-done = f32[512,2,4,128]{3,0,1,2:T(8,128)} async-done(((f32[512,2,1,128]{3,0,1,2:T(8,128)}), f32[512,2,4,128]{3,0,1,2:T(8,128)}) %all-gather.12.cloned.1.call-update) | async-done | bytes 2097168 | tf_op jit(solution)/shard_map/all_gather | solution.py:64
  271.4 84.5 %all-gather.8.cloned.1.call-done = f32[8,512,1024]{2,1,0:T(8,128)} async-done(((f32[1,512,1024]{2,1,0:T(8,128)}), f32[8,512,1024]{2,1,0:T(8,128)}) %all-gather.8.cloned.1.call-update) | async-done | bytes 16777232 | tf_op jit(solution)/shard_map/all_gather | solution.py:11
  363.9 79.2 %all-gather.10.cloned.1.call-done = f32[8,512,1024]{2,1,0:T(8,128)} async-done(((f32[1,512,1024]{2,1,0:T(8,128)}), f32[8,512,1024]{2,1,0:T(8,128)}) %all-gather.10.cloned.1.call-update) | async-done | bytes 16777232 | tf_op jit(solution)/shard_map/all_gather | solution.py:11
  479.3 11.7 %cholesky.222 = f32[128,128]{1,0:T(8,128)S(1)} custom-call(f32[128,128]{1,0:T(8,128)S(1)} %cholesky.577), custom_call_target="Cholesky" | custom-call | tf_op jit(solution)/shard_map/jit(cholesky)/cholesky | solution.py:62
  493.5 9.8 %custom-call.63 = f32[1,128,128]{1,2,0:T(8,128)S(1)} custom-call(f32[1,128,128]{2,1,0:T(8,128)S(1)} %get-tuple-element.72), custom_call_target="InvertDiagBlocksLowerTriangular" | custom-call | tf_op jit(solution)/shard_map/jit(cholesky)/cholesky | solution.py:62
  507.3 11.9 %cholesky.243 = f32[128,128]{1,0:T(8,128)S(1)} custom-call(f32[128,128]{1,0:T(8,128)S(1)} %cholesky.581), custom_call_target="Cholesky" | custom-call | tf_op jit(solution)/shard_map/jit(cholesky)/cholesky | solution.py:62
  519.8 9.8 %custom-call.64 = f32[1,128,128]{1,2,0:T(8,128)S(1)} custom-call(f32[1,128,128]{2,1,0:T(8,128)S(1)} %get-tuple-element.69), custom_call_target="InvertDiagBlocksLowerTriangular" | custom-call | tf_op jit(solution)/shard_map/jit(cholesky)/cholesky | solution.py:62
  533.0 11.7 %cholesky.466 = f32[128,128]{1,0:T(8,128)S(1)} custom-call(f32[128,128]{1,0:T(8,128)S(1)} %cholesky.586), custom_call_target="Cholesky" | custom-call | tf_op jit(solution)/shard_map/jit(cholesky)/cholesky | solution.py:62
  545.9 9.8 %custom-call.65 = f32[1,128,128]{1,2,0:T(8,128)S(1)} custom-call(f32[1,128,128]{2,1,0:T(8,128)S(1)} %get-tuple-element.66), custom_call_target="InvertDiagBlocksLowerTriangular" | custom-call | tf_op jit(solution)/shard_map/jit(cholesky)/cholesky | solution.py:62
  559.3 11.9 %cholesky.485 = f32[128,128]{1,0:T(8,128)S(1)} custom-call(f32[128,128]{1,0:T(8,128)S(1)} %cholesky.591), custom_call_target="Cholesky" | custom-call | tf_op jit(solution)/shard_map/jit(cholesky)/cholesky | solution.py:62
  585.7 11.7 %cholesky.504 = f32[128,128]{1,0:T(8,128)S(1)} custom-call(f32[128,128]{1,0:T(8,128)S(1)} %cholesky.596), custom_call_target="Cholesky" | custom-call | tf_op jit(solution)/shard_map/jit(cholesky)/cholesky | solution.py:62
  598.7 10.2 %custom-call.67 = f32[1,128,128]{1,2,0:T(8,128)S(1)} custom-call(f32[1,128,128]{2,1,0:T(8,128)S(1)} %get-tuple-element.60), custom_call_target="InvertDiagBlocksLowerTriangular" | custom-call | tf_op jit(solution)/shard_map/jit(cholesky)/cholesky | solution.py:62
  612.2 11.7 %cholesky.524 = f32[128,128]{1,0:T(8,128)S(1)} custom-call(f32[128,128]{1,0:T(8,128)S(1)} %cholesky.601), custom_call_target="Cholesky" | custom-call | tf_op jit(solution)/shard_map/jit(cholesky)/cholesky | solution.py:62
  625.2 9.8 %custom-call.68 = f32[1,128,128]{1,2,0:T(8,128)S(1)} custom-call(f32[1,128,128]{2,1,0:T(8,128)S(1)} %get-tuple-element.57), custom_call_target="InvertDiagBlocksLowerTriangular" | custom-call | tf_op jit(solution)/shard_map/jit(cholesky)/cholesky | solution.py:62
  638.0 11.9 %cholesky.544 = f32[128,128]{1,0:T(8,128)S(1)} custom-call(f32[128,128]{1,0:T(8,128)S(1)} %cholesky.606), custom_call_target="Cholesky" | custom-call | tf_op jit(solution)/shard_map/jit(cholesky)/cholesky | solution.py:62
  651.1 9.8 %custom-call.69 = f32[1,128,128]{1,2,0:T(8,128)S(1)} custom-call(f32[1,128,128]{2,1,0:T(8,128)S(1)} %get-tuple-element.54), custom_call_target="InvertDiagBlocksLowerTriangular" | custom-call | tf_op jit(solution)/shard_map/jit(cholesky)/cholesky | solution.py:62
  663.6 11.7 %cholesky.562 = f32[128,128]{1,0:T(8,128)S(1)} custom-call(f32[128,128]{1,0:T(8,128)S(1)} %convolution_subtract_fusion.13), custom_call_target="Cholesky" | custom-call | tf_op jit(solution)/shard_map/jit(cholesky)/cholesky | solution.py:62
  688.1 22.8 %while.1 = (s32[]{:T(128)}, f32[1024,1024]{1,0:T(8,128)}, s32[8,2]{0,1:T(2,128)S(1)}, f32[8,128,128]{2,1,0:T(8,128)S(1)}, s32[]{:T(128)}) while((s32[]{:T(128)}, f32[1024,1024]{1,0:T(8,128)}, s32[8,2]{0,1:T(2,128)S(1)}, f32[8,128,128]{2,1,0:T(8,128)S(1)}, s32[]{:T(128)}) %tuple.68), condition=%wide.while_cond, body=%wide.while_body.sunk | while | flops 2 | bytes 131181 | solution.py:65
  710.9 78.8 %custom-call.70 = f32[8,128,128]{1,2,0:T(8,128)S(1)} custom-call(f32[8,128,128]{2,1,0:T(8,128)S(1)} %get-tuple-element.9), custom_call_target="InvertDiagBlocksLowerTriangular" | custom-call | tf_op jit(solution)/shard_map/jit(_solve_triangular)/triangular_solve | solution.py:65
  823.3 48.1 %all-gather.14.cloned.1.call-done = bf16[4,512,1024]{2,1,0:T(8,128)(2,1)} async-done(((bf16[1,512,1024]{2,1,0:T(8,128)(2,1)}), bf16[4,512,1024]{2,1,0:T(8,128)(2,1)}) %all-gather.14.cloned.1.call-update) | async-done | bytes 4194320 | tf_op jit(solution)/shard_map/all_gather | solution.py:11
  878.7 48.2 %all-gather.16.cloned.1.call-done = bf16[8,4,128,1024]{3,2,1,0:T(8,128)(2,1)} async-done(((bf16[1,4,128,1024]{3,2,1,0:T(8,128)(2,1)}), bf16[8,4,128,1024]{3,2,1,0:T(8,128)(2,1)}) %all-gather.16.cloned.1.call-update) | async-done | bytes 8388624 | tf_op jit(solution)/shard_map/all_gather | solution.py:82
  926.9 10.4 %convolution_bitcast_fusion = f32[512,4,8,128]{0,3,1,2:T(8,128)} fusion(bf16[8,4,128,1024]{3,2,1,0:T(8,128)(2,1)} %all-gather.16.cloned.1.call-done, bf16[384,1024]{1,0:T(8,128)(2,1)S(1)} %get-tuple-element.32, bf16[128,1024]{1,0:T(8,128)(2,1)S(1)} %fusion.36), kind=kOutput, calls=%fused_computation.16 | convolution fusion | flops 4297064448 | bytes 17825792 | tf_op jit(solution)/shard_map/rk,nqbk->rqnb/dot_general | solution.py:79
  937.3 10.4 %copy.78 = f32[512,4,8,128]{3,2,1,0:T(8,128)} copy(f32[512,4,8,128]{0,3,1,2:T(8,128)} %convolution_bitcast_fusion) | data formatting | bytes 16777216 | tf_op jit(solution)/shard_map/rk,nqbk->rqnb/transpose | solution.py:79
  947.7 11.7 %fusion = f32[4,1,128,32,1,128]{5,3,0,2,4,1:T(8,128)} fusion(f32[4,128,32,128]{3,2,0,1:T(8,128)} %copy-done, f32[4,128,32,128]{3,2,1,0:T(8,128)} %bitcast.157, pred[4,32]{1,0:T(4,128)(4,1)S(1)} %broadcast_and_fusion), kind=kLoop, calls=%fused_computation.5 | loop fusion | flops 4194304 | bytes 25165952 | tf_op jit(solution)/shard_map/reshape | solution.py:92
  959.4 11.0 %copy.81 = f32[4,1,128,32,1,128]{5,4,3,2,1,0:T(1,128)} copy(f32[4,1,128,32,1,128]{5,3,0,2,4,1:T(8,128)} %fusion) | data formatting | bytes 16777216
  (157 shorter events, 197.6 us)
Async XLA Ops:
  21.3 37.7 %all-to-all-start.1 = ((s32[128,1,2]{2,1,0:T(1,128)}), s32[128,1,2]{2,1,0:T(1,128)S(1)}, u32[]{:S(2)}, u32[]{:S(2)}) async-start(s32[128,1,2]{2,1,0:T(1,128)} %copy.63), calls=%async_computation.1 | async-start | bytes 131072 | tf_op jit(solution)/shard_map/all_to_all | solution.py:38
  59.1 110.8 %all-to-all-start = ((bf16[128,2,128,128]{3,2,1,0:T(8,128)(2,1)}), bf16[128,2,128,128]{3,2,1,0:T(8,128)(2,1)}, u32[]{:S(2)}, u32[]{:S(2)}) async-start(bf16[128,2,128,128]{3,2,1,0:T(8,128)(2,1)} %scatter_fusion), calls=%async_computation | async-start | bytes 16777216 | tf_op jit(solution)/shard_map/all_to_all | solution.py:37
  69.3 165.9 %all-gather.18.cloned.1.call-start = ((), (), s32[]{:S(2)}) async-start(), calls=%async_computation.7 | async-start | bytes 2228224 | tf_op jit(solution)/shard_map/all_gather | solution.py:54
  187.2 3.4 copy-start
  191.4 77.1 %all-gather.12.cloned.1.call-start = ((), (), s32[]{:S(2)}) async-start(), calls=%async_computation.4 | async-start | bytes 2621440 | tf_op jit(solution)/shard_map/all_gather | solution.py:64
  194.1 161.8 %all-gather.8.cloned.1.call-start = ((), (), s32[]{:S(2)}) async-start(), calls=%async_computation.2 | async-start | bytes 18874368 | tf_op jit(solution)/shard_map/all_gather | solution.py:11
  243.7 199.4 %all-gather.10.cloned.1.call-start = ((), (), s32[]{:S(2)}) async-start(), calls=%async_computation.3 | async-start | bytes 18874368 | tf_op jit(solution)/shard_map/all_gather | solution.py:11
  249.8 621.6 %all-gather.14.cloned.1.call-start = ((), (), s32[]{:S(2)}) async-start(), calls=%async_computation.5 | async-start | bytes 5242880 | tf_op jit(solution)/shard_map/all_gather | solution.py:11
  477.4 1.9 copy-start.1
  682.1 107.6 %copy-start.2 = (f32[512,2,4,128]{0,3,2,1:T(8,128)S(1)}, f32[512,2,4,128]{0,3,2,1:T(8,128)}, u32[]{:S(2)}) copy-start(f32[512,2,4,128]{0,3,2,1:T(8,128)} %copy.69) | copy-start | bytes 6291460
  789.7 8.2 copy-start.3
  823.2 103.7 %all-gather.16.cloned.1.call-start = ((), (), s32[]{:S(2)}) async-start(), calls=%async_computation.6 | async-start | bytes 9437184 | tf_op jit(solution)/shard_map/all_gather | solution.py:82
Sparse Core Ops, SparseCore 0:
  191.5 43.6 all-gather.17
  236.9 31.5 all-gather.11
  270.2 85.6 all-gather.7
  357.5 85.5 all-gather.9
  823.3 48.0 all-gather.13
  876.0 50.7 all-gather.15
